TPU v7x, 256 devices: a whole 4x4x8 slice. The times are simulated.
256 devices in a mesh: row: 16 (over z, core), col: 16 (over x, y).
Axes of the slice: x: 4, y: 4, z: 8, core: 2. Of those that a mesh axis runs over, the one named last changes fastest.
Arguments:
- tensor: float32 [12, 8192, 8192], P(None, 'row', 'col'), may hold values from -6 to 6
- factor_b: float32 [8192, 128], P(('col', 'row')), may hold values from -0.0625 to 0.0625
- factor_c: float32 [12, 128], replicated, may hold values from -1.75 to 1.75
Outputs:
- a_update: float32 [8192, 128], P(('row', 'col'))
- b_update: float32 [8192, 128], P(('col', 'row'))
All inputs are finite; a program needn't handle non-finite values.
Results may differ from a plain program's by a relative error of at most 0.00012.
Values sent between devices are 32-bit elements; how exact they have to be, the bound alone decides.
No kernel may reach another device: no remote copies, remote signals or barrier semaphores. Data moves between devices by JAX's collectives and lax.ppermute only.
A program may use at most 64 MiB of HBM per device.

v0:
```python
import jax
import jax.numpy as jnp
from jax import lax
from jax.sharding import PartitionSpec as P

EPSILON = 1e-06


def solve_system(rhs, system):
    highest = lax.Precision.HIGHEST
    lower = jnp.linalg.cholesky(system)
    inverse = jax.scipy.linalg.cho_solve(
        (lower, True), jnp.eye(system.shape[0], dtype=system.dtype)
    )
    return jnp.dot(rhs, inverse, precision=highest)


def gram_of(matrix):
    return jnp.dot(matrix.T, matrix, precision=lax.Precision.HIGHEST)


def per_device(tensor, factor_b, factor_c):
    highest = lax.Precision.HIGHEST
    rows_block = tensor.shape[1]
    cols_block = tensor.shape[2]
    rank_width = factor_c.shape[1]
    owned_a = rows_block // lax.axis_size("col")
    owned_b = cols_block // lax.axis_size("row")
    c_gram = gram_of(factor_c)
    empty_b = jnp.zeros((cols_block, rank_width), jnp.float32)
    gram_b = lax.psum(gram_of(factor_b), ("row", "col"))
    block = tensor
    khatri = factor_c[:, None, :] * lax.all_gather(factor_b, "row", axis=0, tiled=True)[None, :, :]
    partial_a = jnp.einsum("kij,kjr->ir", block, khatri, precision=highest)
    whole_a = lax.psum(partial_a, "col")
    summed_a = lax.dynamic_slice_in_dim(whole_a, lax.axis_index("col") * owned_a, owned_a, 0)
    a_update = solve_system(summed_a, c_gram * gram_b)
    squares = lax.psum(jnp.sum(a_update * a_update, axis=0), ("row", "col"))
    factor_a = a_update / jnp.sqrt(squares + EPSILON)
    gram_a = lax.psum(gram_of(factor_a), ("row", "col"))
    block = tensor
    khatri = factor_c[:, None, :] * lax.all_gather(factor_a, "col", axis=0, tiled=True)[None, :, :]
    partial_b = empty_b + jnp.einsum("kij,kir->jr", block, khatri, precision=highest)
    whole_b = lax.psum(partial_b, "row")
    summed_b = lax.dynamic_slice_in_dim(whole_b, lax.axis_index("row") * owned_b, owned_b, 0)
    b_update = solve_system(summed_b, c_gram * gram_a)
    return (a_update, b_update)


def solution(mesh):
    placed = (P(None, "row", "col"), P(("col", "row"), None), P())
    return jax.shard_map(
        per_device,
        mesh=mesh,
        in_specs=placed,
        out_specs=(P(("row", "col"), None), P(("col", "row"), None)),
        check_vma=False,
    )
```

profile of v0, /device:TPU:1, one launch (start us, length us, event | category | flops | bytes accessed | tf_op | source)
XLA Modules:
  0.0 809.7 jit_solution(5450451104905007428)
XLA Ops:
  7.2 1.7 fusion.35
  9.0 22.3 %all_gather.6 = f32[512,128]{1,0:T(8,128)S(1)} all-gather(f32[32,128]{1,0:T(8,128)} %param.7), channel_id=1, replica_groups=mesh['row'=16,'col'=16] {'row'}, dimensions={0}, use_global_device_ids=true | all-gather | bytes 278528 | tf_op jit(solution)/shard_map/all_gather | solution.py:33
  31.2 18.3 %fusion.8 = f32[512,128]{0,1:T(8,128)} fusion(f32[12,512,512]{2,1,0:T(8,128)} %param.6, f32[512,128]{1,0:T(8,128)S(1)} %all_gather.6, f32[12,128]{1,0:T(8,128)} %param.8), kind=kOutput, calls=%fused_computation.8 | convolution fusion | flops 4832624640 | bytes 13113344 | tf_op jit(solution)/shard_map/kij,kjr->ir/dot_general | solution.py:34
  49.8 209.2 %all-reduce.7.cloned.1.call-done = f32[128,128]{0,1:T(8,128)} async-done(((f32[128,128]{0,1:T(8,128)}), f32[128,128]{0,1:T(8,128)}) %all-reduce.7.cloned.1.call-update) | async-done | bytes 65552 | tf_op jit(solution)/shard_map/psum | solution.py:31
  259.1 1.1 fusion.34
  260.3 11.7 %cholesky.44 = f32[128,128]{1,0:T(8,128)S(1)} custom-call(f32[128,128]{1,0:T(8,128)S(1)} %fusion.27), custom_call_target="Cholesky" | custom-call | tf_op jit(solution)/shard_map/jit(cholesky)/cholesky | solution.py:11
  272.1 0.6 compare_reduce_fusion.1
  272.7 0.7 fusion.18
  273.4 9.8 %custom-call.8 = f32[1,128,128]{1,2,0:T(8,128)S(1)} custom-call(f32[1,128,128]{2,1,0:T(8,128)S(1)} %fusion.18), custom_call_target="InvertDiagBlocksLowerTriangular" | custom-call | tf_op jit(solution)/shard_map/jit(_cho_solve)/triangular_solve | solution.py:12
  283.2 0.3 fusion.16
  283.7 68.0 %all-reduce.5.cloned.1.call-done = f32[512,128]{0,1:T(8,128)} async-done(((f32[512,128]{0,1:T(8,128)}), f32[512,128]{0,1:T(8,128)}) %all-reduce.5.cloned.1.call-update) | async-done | bytes 262160 | tf_op jit(solution)/shard_map/psum | solution.py:35
  351.7 1.2 multiply_reduce_fusion
  352.8 77.5 %psum.37 = f32[128]{0:T(128)S(1)} all-reduce(f32[128]{0:T(128)S(1)} %get-tuple-element.6), channel_id=1, replica_groups=mesh['row'=16,'col'=16] {'row','col'}, use_global_device_ids=true, to_apply=%region_5.0 | all-reduce | flops 128 | bytes 1024 | tf_op jit(solution)/shard_map/psum | solution.py:38
  430.3 0.9 fusion.36
  431.3 15.8 %all_gather.7 = f32[512,128]{1,0:T(8,128)S(1)} all-gather(f32[32,128]{1,0:T(8,128)S(1)} %broadcast_divide_fusion), channel_id=1, replica_groups=mesh['row'=16,'col'=16] {'col'}, dimensions={0}, use_global_device_ids=true | all-gather | bytes 278528 | tf_op jit(solution)/shard_map/all_gather | solution.py:42
  447.3 11.4 %fusion.11 = f32[512,128]{0,1:T(8,128)} fusion(f32[12,512,512]{2,1,0:T(8,128)} %param.6, f32[512,128]{1,0:T(8,128)S(1)} %all_gather.7, f32[12,128]{1,0:T(8,128)S(1)} %copy-done), kind=kOutput, calls=%fused_computation.9 | convolution fusion | flops 4832624640 | bytes 13113344 | tf_op jit(solution)/shard_map/kij,kir->jr/dot_general | solution.py:43
  458.8 234.0 %all-reduce.11.cloned.1.call-done = f32[128,128]{0,1:T(8,128)} async-done(((f32[128,128]{0,1:T(8,128)}), f32[128,128]{0,1:T(8,128)}) %all-reduce.11.cloned.1.call-update) | async-done | bytes 65552 | tf_op jit(solution)/shard_map/psum | solution.py:40
  692.8 0.9 mul.48
  693.8 11.7 %cholesky.55 = f32[128,128]{1,0:T(8,128)S(1)} custom-call(f32[128,128]{1,0:T(8,128)S(1)} %fusion.23), custom_call_target="Cholesky" | custom-call | tf_op jit(solution)/shard_map/jit(cholesky)/cholesky | solution.py:11
  705.5 0.6 compare_reduce_fusion
  706.2 0.7 fusion.19
  706.8 9.8 %custom-call.9 = f32[1,128,128]{1,2,0:T(8,128)S(1)} custom-call(f32[1,128,128]{2,1,0:T(8,128)S(1)} %fusion.19), custom_call_target="InvertDiagBlocksLowerTriangular" | custom-call | tf_op jit(solution)/shard_map/jit(_cho_solve)/triangular_solve | solution.py:12
  717.2 84.3 %all-reduce.9.cloned.1.call-done = f32[512,128]{0,1:T(8,128)} async-done(((f32[512,128]{0,1:T(8,128)}), f32[512,128]{0,1:T(8,128)}) %all-reduce.9.cloned.1.call-update) | async-done | bytes 262160 | tf_op jit(solution)/shard_map/psum | solution.py:44
  801.4 1.8 fusion.28
  (23 shorter events, 1.6 us)
Async XLA Ops:
  7.2 251.9 %all-reduce.7.cloned.1.call-start = ((), (), s32[]{:S(2)}) async-start(), calls=%async_computation.1 | async-start | bytes 131072 | tf_op jit(solution)/shard_map/psum | solution.py:31
  8.9 342.7 %all-reduce.5.cloned.1.call-start = ((), (), s32[]{:S(2)}) async-start(), calls=%async_computation | async-start | bytes 524288 | tf_op jit(solution)/shard_map/psum | solution.py:35
  31.2 227.8 %copy-start = (f32[12,128]{1,0:T(8,128)S(1)}, f32[12,128]{1,0:T(8,128)}, u32[]{:S(2)}) copy-start(f32[12,128]{1,0:T(8,128)} %param.8) | copy-start | bytes 18436
  49.6 643.2 %all-reduce.11.cloned.1.call-start = ((), (), s32[]{:S(2)}) async-start(), calls=%async_computation.3 | async-start | bytes 131072 | tf_op jit(solution)/shard_map/psum | solution.py:40
  352.8 105.9 %copy-start.1 = (f32[32,128]{1,0:T(8,128)}, f32[32,128]{1,0:T(8,128)S(1)}, u32[]{:S(2)}) copy-start(f32[32,128]{1,0:T(8,128)S(1)} %get-tuple-element.7) | copy-start | bytes 49156
  447.1 354.4 %all-reduce.9.cloned.1.call-start = ((), (), s32[]{:S(2)}) async-start(), calls=%async_computation.2 | async-start | bytes 524288 | tf_op jit(solution)/shard_map/psum | solution.py:44
Sparse Core Ops, SparseCore 0:
  13.5 245.5 all-reduce.6
  262.2 89.3 all-reduce.4
  447.2 245.5 all-reduce.10
  695.0 106.4 all-reduce.8
where the time goes:
time: 810 us
  waiting for transfers between devices  596 us (74%)
  blocking collectives  116 us (14%)
  other arithmetic  46.6 us (6%)
  matrix products  37.4 us (5%)
  between operations  13.9 us (2%)
    psum x1, waiting for transfers between devices, per_device(): gram_a = lax.psum(gram_of(factor_a), ('row', 'col'))  234 us
    psum x1, waiting for transfers between devices, per_device(): gram_b = lax.psum(gram_of(factor_b), ('row', 'col'))  209 us
    psum x1, waiting for transfers between devices, per_device(): whole_b = lax.psum(partial_b, 'row')  84.3 us
    psum x1, blocking collectives, per_device(): squares = lax.psum(jnp.sum(a_update * a_update, axis=0), ('row', 'col'))  77.5 us
    psum x1, waiting for transfers between devices, per_device(): whole_a = lax.psum(partial_a, 'col')  68 us
    another operation x6, other arithmetic, solve_system(): lower = jnp.linalg.cholesky(system)  24.8 us
    all_gather x1, blocking collectives, per_device(): lax.all_gather(factor_b, 'row', axis=0, tiled=True)[None, :, :]  22.3 us
    another operation x4, other arithmetic, solve_system(): jax.scipy.linalg.cho_solve((lower, True), jnp.eye(system.shape[0], dtype=...  20.9 us
  transfers between devices with their start and end apart: 4, of which 4 were waited for; matrix products, arithmetic and copies ran while one was open for 10% of the time, Pallas kernels for 0%

commit v1 on v0

--- a/solution.py
+++ b/solution.py
@@ -37,7 +37,7 @@
     a_update = solve_system(summed_a, c_gram * gram_b)
     squares = lax.psum(jnp.sum(a_update * a_update, axis=0), ("row", "col"))
     factor_a = a_update / jnp.sqrt(squares + EPSILON)
-    gram_a = lax.psum(gram_of(factor_a), ("row", "col"))
+    gram_a = jnp.sum(lax.all_gather(gram_of(factor_a), ("row", "col")), axis=0)
     block = tensor
     khatri = factor_c[:, None, :] * lax.all_gather(factor_a, "col", axis=0, tiled=True)[None, :, :]
     partial_b = empty_b + jnp.einsum("kij,kir->jr", block, khatri, precision=highest)

time: 810 us -> 671 us (0.83)
  waiting for transfers between devices: 596 us -> 452 us
    psum x1 -> x0, waiting for transfers between devices: 234 us -> none  [per_device(): gram_a = lax.psum(gram_of(factor_a), ('row', 'col'))]
    all_gather x0 -> x1, waiting for transfers between devices: none -> 94.3 us  [per_device(): gram_a = jnp.sum(lax.all_gather(gram_of(factor_a), ('row', 'col')), axis=0)]
  transfers between devices with their start and end apart: 4 -> 4, of which waited for: 4 -> 4; matrix products, arithmetic and copies ran while one was open for 10% -> 12% of each run, Pallas kernels for 0% -> 0%
where the time goes in v1:
time: 671 us
  waiting for transfers between devices  452 us (67%)
  blocking collectives  116 us (17%)
  other arithmetic  52.3 us (8%)
  matrix products  36 us (5%)
  between operations  13.9 us (2%)
    psum x1, waiting for transfers between devices, per_device(): gram_b = lax.psum(gram_of(factor_b), ('row', 'col'))  211 us
    all_gather x1, waiting for transfers between devices, per_device(): gram_a = jnp.sum(lax.all_gather(gram_of(factor_a), ('row', 'col')), axis=0)  94.3 us
    psum x1, waiting for transfers between devices, per_device(): whole_b = lax.psum(partial_b, 'row')  78.9 us
    psum x1, blocking collectives, per_device(): squares = lax.psum(jnp.sum(a_update * a_update, axis=0), ('row', 'col'))  77.5 us
    psum x1, waiting for transfers between devices, per_device(): whole_a = lax.psum(partial_a, 'col')  68 us
    another operation x6, other arithmetic, solve_system(): lower = jnp.linalg.cholesky(system)  24.8 us
    all_gather x1, blocking collectives, per_device(): lax.all_gather(factor_b, 'row', axis=0, tiled=True)[None, :, :]  22.3 us
    another operation x4, other arithmetic, solve_system(): jax.scipy.linalg.cho_solve((lower, True), jnp.eye(system.shape[0], dtype=...  20.9 us
  transfers between devices with their start and end apart: 4, of which 4 were waited for; matrix products, arithmetic and copies ran while one was open for 12% of the time, Pallas kernels for 0%

profile of v1, /device:TPU:1, one launch (start us, length us, event | category | flops | bytes accessed | tf_op | source)
XLA Modules:
  0.0 671.0 jit_solution(2305239293389513318)
XLA Ops:
  7.2 1.7 fusion.35
  9.0 22.3 %all_gather.12 = f32[512,128]{1,0:T(8,128)S(1)} all-gather(f32[32,128]{1,0:T(8,128)} %param.7), channel_id=1, replica_groups=mesh['row'=16,'col'=16] {'row'}, dimensions={0}, use_global_device_ids=true | all-gather | bytes 278528 | tf_op jit(solution)/shard_map/all_gather | solution.py:33
  31.3 16.8 %fusion.8 = f32[512,128]{0,1:T(8,128)} fusion(f32[12,512,512]{2,1,0:T(8,128)} %param.6, f32[512,128]{1,0:T(8,128)S(1)} %all_gather.12, f32[12,128]{1,0:T(8,128)} %param.8), kind=kOutput, calls=%fused_computation.8 | convolution fusion | flops 4832624640 | bytes 13113344 | tf_op jit(solution)/shard_map/kij,kjr->ir/dot_general | solution.py:34
  48.3 210.7 %all-reduce.6.cloned.1.call-done = f32[128,128]{0,1:T(8,128)} async-done(((f32[128,128]{0,1:T(8,128)}), f32[128,128]{0,1:T(8,128)}) %all-reduce.6.cloned.1.call-update) | async-done | bytes 65552 | tf_op jit(solution)/shard_map/psum | solution.py:31
  259.1 1.1 fusion.34
  260.3 11.7 %cholesky.44 = f32[128,128]{1,0:T(8,128)S(1)} custom-call(f32[128,128]{1,0:T(8,128)S(1)} %fusion.27), custom_call_target="Cholesky" | custom-call | tf_op jit(solution)/shard_map/jit(cholesky)/cholesky | solution.py:11
  272.1 0.6 compare_reduce_fusion.1
  272.7 0.7 fusion.18
  273.4 9.8 %custom-call.8 = f32[1,128,128]{1,2,0:T(8,128)S(1)} custom-call(f32[1,128,128]{2,1,0:T(8,128)S(1)} %fusion.18), custom_call_target="InvertDiagBlocksLowerTriangular" | custom-call | tf_op jit(solution)/shard_map/jit(_cho_solve)/triangular_solve | solution.py:12
  283.7 68.0 %all-reduce.4.cloned.1.call-done = f32[512,128]{0,1:T(8,128)} async-done(((f32[512,128]{0,1:T(8,128)}), f32[512,128]{0,1:T(8,128)}) %all-reduce.4.cloned.1.call-update) | async-done | bytes 262160 | tf_op jit(solution)/shard_map/psum | solution.py:35
  351.7 1.2 multiply_reduce_fusion
  352.9 77.5 %psum.30 = f32[128]{0:T(128)S(1)} all-reduce(f32[128]{0:T(128)S(1)} %get-tuple-element.6), channel_id=1, replica_groups=mesh['row'=16,'col'=16] {'row','col'}, use_global_device_ids=true, to_apply=%region_5.0 | all-reduce | flops 128 | bytes 1024 | tf_op jit(solution)/shard_map/psum | solution.py:38
  430.3 0.9 fusion.36
  431.3 16.5 %all_gather.13 = f32[512,128]{1,0:T(8,128)S(1)} all-gather(f32[32,128]{1,0:T(8,128)S(1)} %broadcast_divide_fusion), channel_id=1, replica_groups=mesh['row'=16,'col'=16] {'col'}, dimensions={0}, use_global_device_ids=true | all-gather | bytes 278528 | tf_op jit(solution)/shard_map/all_gather | solution.py:42
  447.8 11.4 %fusion.11 = f32[512,128]{0,1:T(8,128)} fusion(f32[12,512,512]{2,1,0:T(8,128)} %param.6, f32[512,128]{1,0:T(8,128)S(1)} %all_gather.13, f32[12,128]{1,0:T(8,128)S(1)} %copy-done), kind=kOutput, calls=%fused_computation.9 | convolution fusion | flops 4832624640 | bytes 13113344 | tf_op jit(solution)/shard_map/kij,kir->jr/dot_general | solution.py:43
  459.3 94.3 %all-gather.3.cloned.1.call-done = f32[32768,128]{1,0:T(8,128)} async-done(((f32[128,128]{1,0:T(8,128)}), f32[32768,128]{1,0:T(8,128)}) %all-gather.3.cloned.1.call-update) | async-done | bytes 16777232 | tf_op jit(solution)/shard_map/all_gather | solution.py:40
  553.6 6.6 reduce_sum.19
  560.4 11.7 %cholesky.55 = f32[128,128]{1,0:T(8,128)S(1)} custom-call(f32[128,128]{1,0:T(8,128)S(1)} %fusion.23), custom_call_target="Cholesky" | custom-call | tf_op jit(solution)/shard_map/jit(cholesky)/cholesky | solution.py:11
  572.1 0.6 compare_reduce_fusion
  572.8 0.7 fusion.19
  573.5 9.8 %custom-call.9 = f32[1,128,128]{1,2,0:T(8,128)S(1)} custom-call(f32[1,128,128]{2,1,0:T(8,128)S(1)} %fusion.19), custom_call_target="InvertDiagBlocksLowerTriangular" | custom-call | tf_op jit(solution)/shard_map/jit(_cho_solve)/triangular_solve | solution.py:12
  583.3 0.3 fusion.14
  583.8 78.9 %all-reduce.8.cloned.1.call-done = f32[512,128]{0,1:T(8,128)} async-done(((f32[512,128]{0,1:T(8,128)}), f32[512,128]{0,1:T(8,128)}) %all-reduce.8.cloned.1.call-update) | async-done | bytes 262160 | tf_op jit(solution)/shard_map/psum | solution.py:44
  662.7 1.8 fusion.28
  (25 shorter events, 1.5 us)
Async XLA Ops:
  7.2 251.9 %copy-start = (f32[12,128]{1,0:T(8,128)S(1)}, f32[12,128]{1,0:T(8,128)}, u32[]{:S(2)}) copy-start(f32[12,128]{1,0:T(8,128)} %param.8) | copy-start | bytes 18436
  7.2 251.9 %all-reduce.6.cloned.1.call-start = ((), (), s32[]{:S(2)}) async-start(), calls=%async_computation.1 | async-start | bytes 131072 | tf_op jit(solution)/shard_map/psum | solution.py:31
  8.9 342.7 %all-reduce.4.cloned.1.call-start = ((), (), s32[]{:S(2)}) async-start(), calls=%async_computation | async-start | bytes 524288 | tf_op jit(solution)/shard_map/psum | solution.py:35
  48.1 505.5 %all-gather.3.cloned.1.call-start = ((), (), s32[]{:S(2)}) async-start(), calls=%async_computation.3 | async-start | bytes 16842752 | tf_op jit(solution)/shard_map/all_gather | solution.py:40
  352.8 207.3 %copy-start.1 = (f32[32,128]{1,0:T(8,128)}, f32[32,128]{1,0:T(8,128)S(1)}, u32[]{:S(2)}) copy-start(f32[32,128]{1,0:T(8,128)S(1)} %get-tuple-element.7) | copy-start | bytes 49156
  431.3 231.4 %all-reduce.8.cloned.1.call-start = ((), (), s32[]{:S(2)}) async-start(), calls=%async_computation.2 | async-start | bytes 524288 | tf_op jit(solution)/shard_map/psum | solution.py:44
Sparse Core Ops, SparseCore 0:
  13.5 245.5 all-reduce.5
  262.2 89.3 all-reduce.3
  431.4 122.1 all-gather.2
  555.7 106.8 all-reduce.7
